TPU v7x, 32 devices: a whole 2x2x4 slice. The times are simulated.
32 devices in a mesh: seq: 8 (over y, x, core), mp: 4 (over z).
Axes of the slice: x: 2, y: 2, z: 4, core: 2. Of those that a mesh axis runs over, the one named last changes fastest.
Arguments:
- queries: bfloat16 [8, 96, 64, 128], P('seq', None, 'mp'), may hold values from -12 to 12
- new_keys: bfloat16 [8, 96, 8, 128], P('seq', None, 'mp'), may hold values from -8 to 8
- new_values: bfloat16 [8, 96, 8, 128], P('seq', None, 'mp'), may hold values from -6 to 6
- pool_keys: bfloat16 [128, 8, 128, 128], P('seq', 'mp'), may hold values from -8 to 8
- pool_values: bfloat16 [128, 8, 128, 128], P('seq', 'mp'), may hold values from -6 to 6
- prefix_len: int32 [8], replicated, may hold values from 1 to 2048, as said below
- page_table: int32 [8, 16], replicated, may hold values from -1 to 127, as said below
- out_weight: bfloat16 [8192, 8192], P('mp'), may hold values from -0.0625 to 0.0625
Outputs:
- attended: bfloat16 [8, 96, 8192], P('seq', None, 'mp')
Inputs may be any that keep to these rules, and one draw needn't show every extreme that they name: Prompt r's prefix holds prefix_len[r] tokens in its first ceil(prefix_len[r] / 128) page-table entries. `page_table`: entry [r, l] is the pool page holding positions l * 128 to l * 128 + 127 of prompt r's prefix; entries past the prefix are -1; no pool page appears twice in the table. Pool page p lies on seq index p // 16; one row of the table names at most 2 pages of one seq index, and some row names exactly 2 pages of some seq index.
All inputs are finite; a program needn't handle non-finite values.
Results may differ from a plain program's by a relative error of at most 0.012.
Values may be sent and summed in bfloat16 or wider, within the bound.
A program may use at most 192 MiB of HBM per device.

v0:
```python
import math

import jax
import jax.numpy as jnp
from jax import lax
from jax.sharding import PartitionSpec as P

SLOTS = 2


def on_device(
    queries, new_keys, new_values, pool_keys, pool_values, prefix_len, page_table, out_weight
):
    reqs, fresh, heads, hd = queries.shape
    pages, kvh, page, _ = pool_keys.shape
    rows, maxp = page_table.shape
    group = heads // kvh
    scale = 1.0 / math.sqrt(hd)
    n_seq = lax.axis_size("seq")
    me = lax.axis_index("seq")
    src = jnp.arange(n_seq, dtype=jnp.int32)
    owned = (page_table >= 0)[None] & (page_table[None] // pages == src[:, None, None])
    rank = jnp.cumsum(owned.astype(jnp.int32), axis=-1) - 1
    pick = owned[:, :, None, :] & (
        rank[:, :, None, :] == jnp.arange(SLOTS, dtype=jnp.int32)[None, None, :, None]
    )
    local = jnp.sum(jnp.where(pick[me], (page_table % pages)[:, None, :], 0), axis=-1)
    room = jnp.clip(
        prefix_len[:, None] - jnp.arange(maxp, dtype=jnp.int32)[None] * page, 0, page
    )
    live = jnp.sum(jnp.where(pick, room[None, :, None, :], 0), axis=-1)
    live = lax.dynamic_slice_in_dim(live, me * reqs, reqs, 1)[:, 0]
    sent = jnp.stack([pool_keys[local], pool_values[local]], axis=1)
    got = lax.all_to_all(sent, "seq", split_axis=0, concat_axis=0, tiled=True)
    keys = got[:, 0].transpose(2, 0, 1, 3, 4).reshape(kvh, -1, hd)
    values = got[:, 1].transpose(2, 0, 1, 3, 4).reshape(kvh, -1, hd)
    seen = (jnp.arange(page, dtype=jnp.int32) < live[..., None]).reshape(1, 1, -1)
    q = queries[0].reshape(fresh, kvh, group, hd).transpose(1, 0, 2, 3).reshape(kvh, -1, hd)
    fk = new_keys[0].transpose(1, 0, 2)
    fv = new_values[0].transpose(1, 0, 2)
    row_c = jnp.arange(fresh * group, dtype=jnp.int32) // group
    causal = (jnp.arange(fresh, dtype=jnp.int32)[None, :] <= row_c[:, None])[None]
    s0 = jnp.einsum("jqd,jkd->jqk", q, keys, preferred_element_type=jnp.float32) * scale
    s1 = jnp.einsum("jqd,jkd->jqk", q, fk, preferred_element_type=jnp.float32) * scale
    s0 = jnp.where(seen, s0, -1e30)
    s1 = jnp.where(causal, s1, -1e30)
    m = jnp.maximum(jnp.max(s0, -1, keepdims=True), jnp.max(s1, -1, keepdims=True))
    w0 = jnp.exp(s0 - m)
    w1 = jnp.exp(s1 - m)
    total = jnp.sum(w0, -1, keepdims=True) + jnp.sum(w1, -1, keepdims=True)
    acc = jnp.einsum(
        "jqk,jkd->jqd", w0.astype(jnp.bfloat16), values, preferred_element_type=jnp.float32
    ) + jnp.einsum(
        "jqk,jkd->jqd", w1.astype(jnp.bfloat16), fv, preferred_element_type=jnp.float32
    )
    attn = (acc / total).astype(jnp.bfloat16)
    attn = attn.reshape(kvh, fresh, group, hd).transpose(1, 0, 2, 3).reshape(fresh, heads * hd)
    part = jnp.dot(attn, out_weight, preferred_element_type=jnp.float32).astype(jnp.bfloat16)
    out = lax.psum_scatter(part, "mp", scatter_dimension=1, tiled=True)
    return out[None]


def solution(mesh):
    in_specs = (
        P("seq", None, "mp", None),
        P("seq", None, "mp", None),
        P("seq", None, "mp", None),
        P("seq", "mp", None, None),
        P("seq", "mp", None, None),
        P(),
        P(),
        P("mp", None),
    )
    return jax.shard_map(
        on_device, mesh=mesh, in_specs=in_specs, out_specs=P("seq", None, "mp"), check_vma=False
    )
```

profile of v0, /device:TPU:1, one launch (start us, length us, event | category | flops | bytes accessed | tf_op | source)
XLA Modules:
  0.0 115.2 jit_solution(17400074746346990850)
XLA Ops:
  6.5 0.8 add_select_fusion.1
  7.3 0.7 broadcast_compare_fusion
  8.1 1.4 %reduce_window_sum.11 = s32[8,8,16]{2,1,0:T(8,128)S(1)} reduce-window(s32[8,8,16]{2,1,0:T(8,128)S(1)} %get-tuple-element.10, s32[]{:T(128)} %constant.55.clone.1), window={size=1x1x16 pad=0_0x0_0x15_0}, to_apply=%region_0.1 | reduce-window | flops 15360 | bytes 8196 | tf_op jit(solution)/shard_map/jit(cumsum)/reduce_window_sum | solution.py:23
  9.4 0.7 subtract_clamp_fusion
  10.1 0.4 select_reduce_fusion
  10.5 0.1 select_reduce_fusion.1
  10.9 0.7 gather_fusion.1
  11.6 2.0 %gather_fusion = bf16[16,2,128,128]{3,2,1,0:T(8,128)(2,1)S(1)} fusion(bf16[16,2,128,128]{3,2,1,0:T(8,128)(2,1)} %param.11, s32[1024]{0:T(1024)S(1)} %pad_clamp_fusion), kind=kCustom, calls=%fused_computation | custom fusion | bytes 2097216 | tf_op jit(solution)/shard_map/gather | solution.py:33
  13.6 0.2 pad_maximum_fusion
  13.8 1.5 %copy.48 = bf16[8,2,2,2,128,128]{5,4,2,3,1,0:T(8,128)(2,1)} copy(bf16[8,2,2,2,128,128]{5,4,3,2,0,1:T(8,128)(2,1)S(1)} %pad_maximum_fusion) | data formatting | bytes 4194304 | tf_op jit(solution)/shard_map/stack | solution.py:33
  15.3 5.2 %all-to-all-start = ((bf16[8,2,2,2,128,128]{5,4,2,3,1,0:T(8,128)(2,1)}), bf16[8,2,2,2,128,128]{5,4,2,3,1,0:T(8,128)(2,1)S(1)}, u32[]{:S(2)}, u32[]{:S(2)}) async-start(bf16[8,2,2,2,128,128]{5,4,2,3,1,0:T(8,128)(2,1)} %copy.48), calls=%async_computation | async-start | bytes 4194304 | tf_op jit(solution)/shard_map/all_to_all | solution.py:34
  20.6 0.1 copy.45
  20.7 0.1 copy.46
  20.9 2.5 %fusion.34 = (f32[2,768]{1,0:T(2,128)}, f32[2,768,96]{1,2,0:T(8,128)}) fusion(bf16[2,96,128]{2,0,1:T(2,128)(2,1)} %bitcast.71, pred[768,96]{0,1:T(8,128)(4,1)S(1)} %iota_compare_fusion, bf16[1,96,16,128]{3,2,1,0:T(8,128)(2,1)S(1)} %copy-done.2), kind=kOutput, calls=%fused_computation.66 | convolution fusion | flops 38189568 | bytes 1112064 | tf_op jit(solution)/shard_map/jqd,jkd->jqk/dot_general | solution.py:44
  23.4 20.3 %all-to-all-done = bf16[8,2,2,2,128,128]{5,4,2,3,1,0:T(8,128)(2,1)S(1)} async-done(((bf16[8,2,2,2,128,128]{5,4,2,3,1,0:T(8,128)(2,1)}), bf16[8,2,2,2,128,128]{5,4,2,3,1,0:T(8,128)(2,1)S(1)}, u32[]{:S(2)}, u32[]{:S(2)}) %all-to-all-start) | async-done | bytes 2097184 | tf_op jit(solution)/shard_map/all_to_all | solution.py:34
  43.7 0.1 slice_bitcast_fusion.1
  43.8 0.1 copy.52
  44.0 1.9 %bitcast_reduce_fusion = (f32[2,768]{1,0:T(2,128)S(1)}, f32[2,2048,768]{2,1,0:T(8,128)S(1)}) fusion(pred[2048]{0:T(1024)(128)(4,1)S(1)} %lt.48, bf16[2,2048,128]{2,1,0:T(8,128)(2,1)S(1)} %bitcast.67, bf16[1,96,16,128]{3,2,1,0:T(8,128)(2,1)S(1)} %copy-done.2), kind=kOutput, calls=%fused_computation.3 | convolution fusion | flops 814742016 | bytes 14032896 | tf_op jit(solution)/shard_map/jqd,jkd->jqk/dot_general | solution.py:43
  46.0 3.4 %fusion.1 = f32[2,768]{1,0:T(2,128)S(1)} fusion(f32[2,2048,768]{2,1,0:T(8,128)S(1)} %get-tuple-element.14, f32[2,768]{1,0:T(2,128)S(1)} %max.12, pred[2048]{0:T(1024)(128)(4,1)S(1)} %lt.48), kind=kLoop, calls=%fused_computation.6 | loop fusion | flops 12581376 | bytes 12597248 | tf_op jit(solution)/shard_map/reduce_sum | solution.py:50
  49.4 5.0 %fusion.3 = f32[2,768,128]{2,1,0:T(8,128)} fusion(bf16[2,2048,128]{2,1,0:T(8,128)(2,1)S(1)} %bitcast.69, f32[2,2048,768]{2,1,0:T(8,128)S(1)} %get-tuple-element.14, f32[2,768]{1,0:T(2,128)S(1)} %max.12, pred[2048]{0:T(1024)(128)(4,1)S(1)} %lt.48), kind=kOutput, calls=%fused_computation.9 | convolution fusion | flops 817889280 | bytes 14426112 | tf_op jit(solution)/shard_map/jqk,jkd->jqd/dot_general | solution.py:51
  54.3 0.1 fusion.10
  54.5 1.5 %fusion.9 = bf16[2,96,8,128]{3,2,1,0:T(8,128)(2,1)S(1)} fusion(f32[2,768,128]{2,1,0:T(8,128)} %fusion.3, f32[2,768]{1,0:T(2,128)S(1)} %add.50, f32[2,768,96]{1,2,0:T(8,128)S(1)} %copy-done.1, f32[2,768]{1,0:T(2,128)S(1)} %max.12, bf16[2,96,128]{2,0,1:T(2,128)(2,1)S(1)} %bitcast.72), kind=kOutput, calls=%fused_computation.17 | convolution fusion | flops 38633472 | bytes 1830912 | tf_op jit(solution)/shard_map/jqk,jkd->jqd/dot_general | solution.py:53
  56.1 14.7 %convolution_convert_fusion = bf16[96,8192]{1,0:T(8,128)(2,1)} fusion(bf16[2048,8192]{1,0:T(8,128)(2,1)} %param.15, bf16[12,8,16,128]{3,2,1,0:T(8,128)(2,1)S(1)} %bitcast.68), kind=kOutput, calls=%fused_computation.8 | convolution fusion | flops 3222011904 | bytes 35520512 | tf_op jit(solution)/shard_map/dot_general | solution.py:58
  70.8 37.5 %reduce-scatter.2.cloned.1.call-done = bf16[96,2048]{1,0:T(8,128)(2,1)} async-done(((bf16[96,8192]{1,0:T(8,128)(2,1)}), bf16[96,2048]{1,0:T(8,128)(2,1)}) %reduce-scatter.2.cloned.1.call-update) | async-done | bytes 393232 | tf_op jit(solution)/shard_map/reduce_scatter | solution.py:59
  (28 shorter events, 0.6 us)
Async XLA Ops:
  6.5 4.3 %copy-start = (bf16[16,2,128,128]{3,2,1,0:T(8,128)(2,1)S(1)}, bf16[16,2,128,128]{3,2,1,0:T(8,128)(2,1)}, u32[]{:S(2)}) copy-start(bf16[16,2,128,128]{3,2,1,0:T(8,128)(2,1)} %param.12) | copy-start | bytes 3145732
  6.5 14.4 %copy-start.2 = (bf16[1,96,16,128]{3,2,1,0:T(8,128)(2,1)S(1)}, bf16[1,96,16,128]{3,2,1,0:T(8,128)(2,1)}, u32[]{:S(2)}) copy-start(bf16[1,96,16,128]{3,2,1,0:T(8,128)(2,1)} %param.8) | copy-start | bytes 1179652
  15.3 28.4 %all-to-all-start = ((bf16[8,2,2,2,128,128]{5,4,2,3,1,0:T(8,128)(2,1)}), bf16[8,2,2,2,128,128]{5,4,2,3,1,0:T(8,128)(2,1)S(1)}, u32[]{:S(2)}, u32[]{:S(2)}) async-start(bf16[8,2,2,2,128,128]{5,4,2,3,1,0:T(8,128)(2,1)} %copy.48), calls=%async_computation | async-start | bytes 4194304 | tf_op jit(solution)/shard_map/all_to_all | solution.py:34
  20.5 87.8 %reduce-scatter.2.cloned.1.call-start = ((), (), s32[]{:S(2)}) async-start(), calls=%async_computation.2 | async-start | bytes 1966080 | tf_op jit(solution)/shard_map/reduce_scatter | solution.py:59
  43.7 2.3 %copy-start.3 = (f32[2,768]{1,0:T(2,128)S(1)}, f32[2,768]{1,0:T(2,128)}, u32[]{:S(2)}) copy-start(f32[2,768]{1,0:T(2,128)} %get-tuple-element.15) | copy-start | bytes 18436
  49.4 5.0 %copy-start.1 = (f32[2,768,96]{1,2,0:T(8,128)S(1)}, f32[2,768,96]{1,2,0:T(8,128)}, u32[]{:S(2)}) copy-start(f32[2,768,96]{1,2,0:T(8,128)} %get-tuple-element.16) | copy-start | bytes 1769476
  49.4 5.1 %copy-start.4 = (bf16[1,96,2,128]{3,2,1,0:T(2,128)(2,1)S(1)}, bf16[1,96,2,128]{3,2,1,0:T(2,128)(2,1)}, u32[]{:S(2)}) copy-start(bf16[1,96,2,128]{3,2,1,0:T(2,128)(2,1)} %param.10) | copy-start | bytes 147460
Sparse Core Ops, SparseCore 0:
  71.0 37.2 reduce-scatter.1
where the time goes:
time: 116 us; the launch traced here: 115 us
  waiting for transfers between devices  57.8 us (50%)
  matrix products  25.6 us (22%)
  between operations  13.6 us (12%)
  other arithmetic  7.94 us (7%)
  starting transfers between devices  5.23 us (5%)
  local copies, waits for them, and re-layouts  5.05 us (4%)
    reduce_scatter x1, waiting for transfers between devices, on_device(): out = lax.psum_scatter(part, 'mp', scatter_dimension=1, tiled=True)  37.5 us
    all_to_all x1, waiting for transfers between devices, on_device(): got = lax.all_to_all(sent, 'seq', split_axis=0, concat_axis=0, tiled=True)  20.3 us
    dot_general x1, matrix products, on_device(): jnp.dot(attn, out_weight, preferred_element_type=jnp.float32)  14.7 us
    all_to_all x1, starting transfers between devices, on_device(): got = lax.all_to_all(sent, 'seq', split_axis=0, concat_axis=0, tiled=True)  5.22 us
    dot_general x1, matrix products, on_device(): jnp.einsum('jqk,jkd->jqd', w0.astype(jnp.bfloat16), values, preferred_ele...  4.95 us
    reduce_sum x2, other arithmetic, on_device(): total = jnp.sum(w0, -1, keepdims=True) + jnp.sum(w1, -1, keepdims=True)  3.48 us
    gather x2, local copies, waits for them, and re-layouts, on_device(): sent = jnp.stack([pool_keys[local], pool_values[local]], axis=1)  2.72 us
    dot_general x1, matrix products, on_device(): jnp.einsum('jqd,jkd->jqk', q, fk, preferred_element_type=jnp.float32)  2.48 us
  transfers between devices with their start and end apart: 2, of which 2 were waited for; matrix products, arithmetic and copies ran while one was open for 2% of the time, Pallas kernels for 0%

commit v1 on v0

v1 whole, which is shorter than its diff:
```python
import functools
import math

import jax
import jax.numpy as jnp
from jax import lax
from jax.experimental import pallas as pl
from jax.experimental.pallas import tpu as pltpu
from jax.sharding import PartitionSpec as P

MESH = pl.DeviceIdType.MESH
SLOTS = 2
FLOOR = -1e30


def flipped(index, mask):
    out, bit = index, 1
    while bit <= mask:
        if mask & bit:
            out = out + bit - 2 * bit * ((index // bit) % 2)
        bit *= 2
    return out


def low_bit(r):
    return r & -r


def kernel(
    dims, len_ref, table_ref, q_ref, nk_ref, nv_ref, pk_ref, pv_ref, w_hbm, out_ref,
    wbuf, qs, sendk, sendv, recvk, recvv, probs, peaks, sums, acc, attn, sbuf, rbuf,
    w_sem, ks_sem, kr_sem, vs_sem, vr_sem, rs_sem, rr_sem,
):
    n, n_mp, order, tiles, width = dims
    fresh = q_ref.shape[0]
    pages, kvh, page, hd = pk_ref.shape
    maxp = table_ref.shape[1]
    group = q_ref.shape[1] // hd // kvh
    lanes = group * fresh
    me = lax.axis_index("seq")
    mz = lax.axis_index("mp")
    coef = math.log2(math.e) / math.sqrt(hd)

    def w_copy(pos, t):
        col = pl.multiple_of((flipped(mz, order[pos]) * tiles + t) * width, 128)
        i = pos * tiles + t
        return pltpu.make_async_copy(w_hbm.at[:, pl.ds(col, width)], wbuf.at[i], w_sem.at[i])

    for pos in range(n_mp):
        for t in range(tiles):
            w_copy(pos, t).start()

    steps = []
    bit = 1
    while bit < n_mp:
        steps.append(bit)
        bit *= 2
    barrier = pltpu.get_barrier_semaphore()
    for k in range(1, n):
        pl.semaphore_signal(
            barrier, inc=1, device_id={"seq": lax.rem(me + k, n)}, device_id_type=MESH
        )
    for bit in steps:
        pl.semaphore_signal(
            barrier, inc=1, device_id={"mp": flipped(mz, bit)}, device_id_type=MESH
        )
    pl.semaphore_wait(barrier, n - 1 + len(steps))

    def scan(row, owner):
        first, count = owner * pages, 0
        ids = [0] * SLOTS
        live = [0] * SLOTS
        length = len_ref[row]
        for l in range(maxp):
            p = table_ref[row, l]
            owned = (p >= first) & (p < first + pages)
            room = jnp.clip(length - l * page, 0, page)
            for s in range(SLOTS):
                here = owned & (count == s)
                ids[s] = jnp.where(here, p - first, ids[s])
                live[s] = jnp.where(here, room, live[s])
            count = count + owned.astype(jnp.int32)
        return ids, live

    def page_copy(send, recv, s_sem, r_sem, k, slot, target):
        return pltpu.make_async_remote_copy(
            src_ref=send.at[k], dst_ref=recv.at[slot], send_sem=s_sem.at[k],
            recv_sem=r_sem.at[slot], device_id={"seq": target}, device_id_type=MESH,
        )

    def send_all(pool, send, recv, s_sem, r_sem):
        def one(k, _):
            target = lax.rem(me + k, n)
            ids, _ = scan(target, me)
            for s in range(SLOTS):
                for j in range(kvh):
                    send[k, j, s] = pool[ids[s], j]
            page_copy(send, recv, s_sem, r_sem, k, me, target).start()
            return 0

        lax.fori_loop(1, n, one, 0)
        ids, _ = scan(me, me)
        for s in range(SLOTS):
            for j in range(kvh):
                recv[me, j, s] = pool[ids[s], j]

    send_all(pk_ref, sendk, recvk, ks_sem, kr_sem)
    send_all(pv_ref, sendv, recvv, vs_sem, vr_sem)

    for h in range(kvh * group):
        j, g = h // group, h % group
        qs[j, g * fresh:(g + 1) * fresh, :] = q_ref[:, h * hd:(h + 1) * hd]

    def scores(keys, j):
        return lax.dot_general(
            keys, qs[j], (((1,), (1,)), ((), ())), preferred_element_type=jnp.float32
        )

    def mixed(values, weights):
        return lax.dot_general(
            values, weights, (((0,), (0,)), ((), ())), preferred_element_type=jnp.float32
        )

    lane = lax.broadcasted_iota(jnp.int32, (fresh, lanes), 1)
    token = lane
    for g in range(1, group):
        token = token - jnp.where(lane >= g * fresh, fresh, 0)
    causal = lax.broadcasted_iota(jnp.int32, (fresh, lanes), 0) <= token
    for j in range(kvh):
        s = jnp.where(causal, scores(nk_ref[:, j * hd:(j + 1) * hd], j), FLOOR)
        m = jnp.max(s, axis=0, keepdims=True)
        w = jnp.exp2((s - m) * coef)
        peaks[n, j] = m
        sums[n, j] = jnp.sum(w, axis=0, keepdims=True)
        acc[j] = mixed(nv_ref[:, j * hd:(j + 1) * hd], w.astype(jnp.bfloat16))

    def score_block(k, _):
        src = lax.rem(me + n - k, n)

        @pl.when(k > 0)
        def _():
            page_copy(sendk, recvk, ks_sem, kr_sem, k, src, src).wait_recv()

        _, live = scan(me, src)
        row = lax.broadcasted_iota(jnp.int32, (SLOTS * page, lanes), 0)
        allowed = row < live[0]
        for s in range(1, SLOTS):
            allowed = allowed | ((row >= s * page) & (row < s * page + live[s]))
        for j in range(kvh):
            s = scores(recvk[src, j].reshape(SLOTS * page, hd), j)
            s = jnp.where(allowed, s, FLOOR)
            m = jnp.max(s, axis=0, keepdims=True)
            w = jnp.exp2((s - m) * coef)
            peaks[k, j] = m
            sums[k, j] = jnp.sum(w, axis=0, keepdims=True)
            probs[k, j] = w.astype(jnp.bfloat16)
        return 0

    lax.fori_loop(0, n, score_block, 0)

    tops = []
    for j in range(kvh):
        top = peaks[n, j]
        for k in range(n):
            top = jnp.maximum(top, peaks[k, j])
        total = jnp.zeros_like(top)
        for k in range(n + 1):
            total = total + sums[k, j] * jnp.exp2((peaks[k, j] - top) * coef)
        acc[j] = acc[j] * jnp.exp2((peaks[n, j] - top) * coef)
        sums[n, j] = total
        peaks[n, j] = top

    def value_block(k, _):
        src = lax.rem(me + n - k, n)

        @pl.when(k > 0)
        def _():
            page_copy(sendv, recvv, vs_sem, vr_sem, k, src, src).wait_recv()

        for j in range(kvh):
            part = mixed(recvv[src, j].reshape(SLOTS * page, hd), probs[k, j])
            acc[j] = acc[j] + part * jnp.exp2((peaks[k, j] - peaks[n, j]) * coef)
        return 0

    lax.fori_loop(0, n, value_block, 0)

    for j in range(kvh):
        heads = (acc[j] / sums[n, j]).T.astype(jnp.bfloat16)
        for g in range(group):
            h = j * group + g
            attn[:, h * hd:(h + 1) * hd] = heads[g * fresh:(g + 1) * fresh, :]

    def sum_copy(r, t):
        return pltpu.make_async_remote_copy(
            src_ref=sbuf.at[r, t], dst_ref=rbuf.at[r, t], send_sem=rs_sem.at[r, t],
            recv_sem=rr_sem.at[r, t], device_id={"mp": flipped(mz, low_bit(r))},
            device_id_type=MESH,
        )

    for pos, r in enumerate(order):
        def project(t, _, pos=pos, r=r):
            i = pos * tiles + t
            pltpu.make_async_copy(
                w_hbm.at[:, pl.ds(0, width)], wbuf.at[i], w_sem.at[i]
            ).wait()
            part = jnp.dot(attn[...], wbuf[i], preferred_element_type=jnp.float32)
            if r:
                for bit in steps:
                    if bit < low_bit(r):
                        sum_copy(r + bit, t).wait_recv()
                        part = part + rbuf[r + bit, t].astype(jnp.float32)
            sbuf[r, t] = part.astype(jnp.bfloat16)
            if r:
                sum_copy(r, t).start()
            return 0

        lax.fori_loop(0, tiles, project, 0)

    for t in range(tiles):
        part = sbuf[0, t].astype(jnp.float32)
        for bit in steps:
            sum_copy(bit, t).wait_recv()
            part = part + rbuf[bit, t].astype(jnp.float32)
        out_ref[:, t * width:(t + 1) * width] = part.astype(out_ref.dtype)

    def drain(k, _):
        target = lax.rem(me + k, n)
        page_copy(sendk, recvk, ks_sem, kr_sem, k, me, target).wait_send()
        page_copy(sendv, recvv, vs_sem, vr_sem, k, me, target).wait_send()
        return 0

    lax.fori_loop(1, n, drain, 0)
    for r in range(1, n_mp):
        for t in range(tiles):
            sum_copy(r, t).wait_send()


def on_device(
    n, n_mp, queries, new_keys, new_values, pool_keys, pool_values, prefix_len, page_table, out_weight
):
    reqs, fresh, heads, hd = queries.shape
    pages, kvh, page, _ = pool_keys.shape
    lanes = heads // kvh * fresh
    depth, model = out_weight.shape
    chunk = model // n_mp
    width = min(512, chunk)
    tiles = chunk // width
    order = sorted(range(n_mp), key=lambda r: (low_bit(r) if r else n_mp, -r))
    bf16, f32 = jnp.bfloat16, jnp.float32
    dma = pltpu.SemaphoreType.DMA
    vmem = pl.BlockSpec(memory_space=pltpu.VMEM)
    smem = pl.BlockSpec(memory_space=pltpu.SMEM)
    pages_shape = (n, kvh, SLOTS, page, hd)
    out = pl.pallas_call(
        functools.partial(kernel, (n, n_mp, tuple(order), tiles, width)),
        out_shape=jax.ShapeDtypeStruct((fresh, chunk), bf16),
        in_specs=[smem, smem] + [vmem] * 5 + [pl.BlockSpec(memory_space=pl.ANY)],
        out_specs=vmem,
        scratch_shapes=[
            pltpu.VMEM((n_mp * tiles, depth, width), bf16),
            pltpu.VMEM((kvh, lanes, hd), bf16),
            pltpu.VMEM(pages_shape, bf16),
            pltpu.VMEM(pages_shape, bf16),
            pltpu.VMEM(pages_shape, bf16),
            pltpu.VMEM(pages_shape, bf16),
            pltpu.VMEM((n, kvh, SLOTS * page, lanes), bf16),
            pltpu.VMEM((n + 1, kvh, 1, lanes), f32),
            pltpu.VMEM((n + 1, kvh, 1, lanes), f32),
            pltpu.VMEM((kvh, hd, lanes), f32),
            pltpu.VMEM((fresh, depth), bf16),
            pltpu.VMEM((n_mp, tiles, fresh, width), bf16),
            pltpu.VMEM((n_mp, tiles, fresh, width), bf16),
            dma((n_mp * tiles,)),
            dma((n,)), dma((n,)), dma((n,)), dma((n,)),
            dma((n_mp, tiles)), dma((n_mp, tiles)),
        ],
        compiler_params=pltpu.CompilerParams(
            collective_id=0, has_side_effects=True, vmem_limit_bytes=60 * 2**20
        ),
    )(
        prefix_len,
        page_table,
        queries.reshape(fresh, heads * hd),
        new_keys.reshape(fresh, kvh * hd),
        new_values.reshape(fresh, kvh * hd),
        pool_keys,
        pool_values,
        out_weight,
    )
    return out[None]


def solution(mesh):
    in_specs = (
        P("seq", None, "mp", None),
        P("seq", None, "mp", None),
        P("seq", None, "mp", None),
        P("seq", "mp", None, None),
        P("seq", "mp", None, None),
        P(),
        P(),
        P("mp", None),
    )
    body = functools.partial(on_device, mesh.shape["seq"], mesh.shape["mp"])
    return jax.shard_map(
        body, mesh=mesh, in_specs=in_specs, out_specs=P("seq", None, "mp"), check_vma=False
    )
```

time: 116 us -> 65.1 us (0.56)
  Pallas kernels: 0 us -> 59.7 us
  waiting for transfers between devices: 57.8 us -> 0 us
  matrix products: 25.6 us -> 0 us
  between operations: 13.6 us -> 0.01 us
  other arithmetic: 7.94 us -> 0 us
  starting transfers between devices: 5.23 us -> 0 us
    pallas_call x0 -> x1, Pallas kernels: none -> 59.7 us  [on_device(): pl.pallas_call(functools.partial(kernel, (n, n_mp, tuple(order), tiles, w...]
    reduce_scatter x1 -> x0, waiting for transfers between devices: 37.5 us -> none  [on_device(): out = lax.psum_scatter(part, 'mp', scatter_dimension=1, tiled=True)]
    dot_general x5 -> x0, matrix products: 25.6 us -> none  [the longest x1 14.7 us: on_device(): jnp.dot(attn, out_weight, preferred_element_type=jnp.float32)]
    all_to_all x1 -> x0, waiting for transfers between devices: 20.3 us -> none  [on_device(): got = lax.all_to_all(sent, 'seq', split_axis=0, concat_axis=0, tiled=True)]
    all_to_all x1 -> x0, starting transfers between devices: 5.22 us -> none  [on_device(): got = lax.all_to_all(sent, 'seq', split_axis=0, concat_axis=0, tiled=True)]
    reduce_sum x4 -> x0, other arithmetic: 3.99 us -> none  [the longest x2 3.48 us: on_device(): total = jnp.sum(w0, -1, keepdims=True) + jnp.sum(w1, -1, keepdims=True)]
    unnamed x10 -> x2, local copies, waits for them, and re-layouts: 0.02 us -> 3.61 us
    gather x2 -> x0, local copies, waits for them, and re-layouts: 2.72 us -> none  [on_device(): sent = jnp.stack([pool_keys[local], pool_values[local]], axis=1)]
  transfers between devices with their start and end apart: 2 -> 0, of which waited for: 2 -> 0; matrix products, arithmetic and copies ran while one was open for 2% -> 0% of each run, Pallas kernels for 0% -> 0%
where the time goes in v1:
time: 65.1 us; the launch traced here: 64.8 us
  Pallas kernels  59.7 us (92%)
  local copies, waits for them, and re-layouts  5.08 us (8%)
    pallas_call x1, Pallas kernels, on_device(): pl.pallas_call(functools.partial(kernel, (n, n_mp, tuple(order), tiles, w...  59.7 us
    unnamed x2, local copies, waits for them, and re-layouts  3.61 us
    reshape x1, local copies, waits for them, and re-layouts, on_device(): new_values.reshape(fresh, kvh * hd)  1.47 us

profile of v1, /device:TPU:1, one launch (start us, length us, event | category | flops | bytes accessed | tf_op | source)
XLA Modules:
  0.0 64.8 jit_solution(8576318545021116006)
XLA Ops:
  0.0 1.5 %copy_bitcast_fusion.1 = (bf16[96,256]{1,0:T(8,128)(2,1)}, bf16[96,256]{1,0:T(8,128)(2,1)}) fusion(bf16[12,8,2,128]{3,2,1,0:T(2,128)(2,1)} %bitcast.17, bf16[12,8,2,128]{3,2,1,0:T(2,128)(2,1)} %bitcast.18), kind=kLoop, calls=%fused_computation.1 | loop fusion | bytes 196608 | tf_op jit(solution)/shard_map/reshape | solution.py:285
  1.5 1.8 %copy.15 = bf16[12,8,16,128]{3,1,2,0:T(8,128)(2,1)} copy(bf16[12,8,16,128]{3,2,1,0:T(8,128)(2,1)} %bitcast.16) | data formatting | bytes 786432
  3.3 59.7 %shard_map.82 = bf16[96,2048]{1,0:T(8,128)(2,1)} custom-call(s32[8]{0:T(128)} %len_ref.1, s32[8,16]{1,0:T(8,128)} %table_ref.1, bf16[96,2048]{1,0:T(8,128)(2,1)} %bitcast.15, bf16[96,256]{1,0:T(8,128)(2,1)} %get-tuple-element.6.nk_ref, bf16[96,256]{1,0:T(8,128)(2,1)} %get-tuple-element.5.nv_ref, bf16[16,2,128,128]{3,2,1,0:T(8,128)(2,1)} %pk_ref.1, ...), custom_call_target="tpu_custom_call" | custom-call | tf_op jit(solution)/shard_map/pallas_call | solution.py:254
  63.0 1.8 %copy.17 = bf16[1,96,2048]{2,1,0:T(8,128)(2,1)} copy(bf16[1,96,2048]{2,1,0:T(8,128)(2,1)} %bitcast.14) | data formatting | bytes 786432

commit v2 on v1

--- a/solution.py
+++ b/solution.py
@@ -28,14 +28,14 @@
 
 def kernel(
     dims, len_ref, table_ref, q_ref, nk_ref, nv_ref, pk_ref, pv_ref, w_hbm, out_ref,
-    wbuf, qs, sendk, sendv, recvk, recvv, probs, peaks, sums, acc, attn, sbuf, rbuf,
+    wbuf, q32, n32, qs, sendk, sendv, recvk, recvv, probs, peaks, sums, acc, attn, sbuf, rbuf,
     w_sem, ks_sem, kr_sem, vs_sem, vr_sem, rs_sem, rr_sem,
 ):
     n, n_mp, order, tiles, width = dims
-    fresh = q_ref.shape[0]
+    fresh = q_ref.shape[1]
     pages, kvh, page, hd = pk_ref.shape
     maxp = table_ref.shape[1]
-    group = q_ref.shape[1] // hd // kvh
+    group = q_ref.shape[2] // kvh
     lanes = group * fresh
     me = lax.axis_index("seq")
     mz = lax.axis_index("mp")
@@ -88,14 +88,15 @@
             recv_sem=r_sem.at[slot], device_id={"seq": target}, device_id_type=MESH,
         )
 
-    def send_all(pool, send, recv, s_sem, r_sem):
+    def send_all(pool, send, recv, start):
         def one(k, _):
             target = lax.rem(me + k, n)
             ids, _ = scan(target, me)
             for s in range(SLOTS):
                 for j in range(kvh):
                     send[k, j, s] = pool[ids[s], j]
-            page_copy(send, recv, s_sem, r_sem, k, me, target).start()
+            if start:
+                page_copy(send, recv, ks_sem, kr_sem, k, me, target).start()
             return 0
 
         lax.fori_loop(1, n, one, 0)
@@ -104,12 +105,15 @@
             for j in range(kvh):
                 recv[me, j, s] = pool[ids[s], j]
 
-    send_all(pk_ref, sendk, recvk, ks_sem, kr_sem)
-    send_all(pv_ref, sendv, recvv, vs_sem, vr_sem)
-
+    send_all(pk_ref, sendk, recvk, True)
+    send_all(pv_ref, sendv, recvv, False)
+
+    q32[...] = q_ref[0].astype(jnp.float32)
+    n32[0] = nk_ref[0].astype(jnp.float32)
+    n32[1] = nv_ref[0].astype(jnp.float32)
     for h in range(kvh * group):
         j, g = h // group, h % group
-        qs[j, g * fresh:(g + 1) * fresh, :] = q_ref[:, h * hd:(h + 1) * hd]
+        qs[j, g * fresh:(g + 1) * fresh, :] = q32[:, h, :].astype(jnp.bfloat16)
 
     def scores(keys, j):
         return lax.dot_general(
@@ -127,12 +131,20 @@
         token = token - jnp.where(lane >= g * fresh, fresh, 0)
     causal = lax.broadcasted_iota(jnp.int32, (fresh, lanes), 0) <= token
     for j in range(kvh):
-        s = jnp.where(causal, scores(nk_ref[:, j * hd:(j + 1) * hd], j), FLOOR)
+        s = jnp.where(causal, scores(n32[0, :, j, :].astype(jnp.bfloat16), j), FLOOR)
         m = jnp.max(s, axis=0, keepdims=True)
         w = jnp.exp2((s - m) * coef)
         peaks[n, j] = m
         sums[n, j] = jnp.sum(w, axis=0, keepdims=True)
-        acc[j] = mixed(nv_ref[:, j * hd:(j + 1) * hd], w.astype(jnp.bfloat16))
+        acc[j] = mixed(n32[1, :, j, :].astype(jnp.bfloat16), w.astype(jnp.bfloat16))
+
+    def send_values(k, _):
+        target = lax.rem(me + k, n)
+        page_copy(sendk, recvk, ks_sem, kr_sem, k, me, target).wait_send()
+        page_copy(sendv, recvv, vs_sem, vr_sem, k, me, target).start()
+        return 0
+
+    lax.fori_loop(1, n, send_values, 0)
 
     def score_block(k, _):
         src = lax.rem(me + n - k, n)
@@ -225,7 +237,6 @@
 
     def drain(k, _):
         target = lax.rem(me + k, n)
-        page_copy(sendk, recvk, ks_sem, kr_sem, k, me, target).wait_send()
         page_copy(sendv, recvv, vs_sem, vr_sem, k, me, target).wait_send()
         return 0
 
@@ -258,6 +269,8 @@
         out_specs=vmem,
         scratch_shapes=[
             pltpu.VMEM((n_mp * tiles, depth, width), bf16),
+            pltpu.VMEM((fresh, heads, hd), f32),
+            pltpu.VMEM((2, fresh, kvh, hd), f32),
             pltpu.VMEM((kvh, lanes, hd), bf16),
             pltpu.VMEM(pages_shape, bf16),
             pltpu.VMEM(pages_shape, bf16),
@@ -280,9 +293,9 @@
     )(
         prefix_len,
         page_table,
-        queries.reshape(fresh, heads * hd),
-        new_keys.reshape(fresh, kvh * hd),
-        new_values.reshape(fresh, kvh * hd),
+        queries,
+        new_keys,
+        new_values,
         pool_keys,
         pool_values,
         out_weight,

time: 65.1 us -> 61.7 us (0.948)
  local copies, waits for them, and re-layouts: 5.08 us -> 1.77 us
    unnamed x2 -> x1, local copies, waits for them, and re-layouts: 3.61 us -> 1.77 us
    reshape x1 -> x0, local copies, waits for them, and re-layouts: 1.47 us -> none  [on_device(): new_values.reshape(fresh, kvh * hd)]
where the time goes in v2:
time: 61.7 us; the launch traced here: 61.5 us
  Pallas kernels  59.7 us (97%)
  local copies, waits for them, and re-layouts  1.77 us (3%)
    pallas_call x1, Pallas kernels, on_device(): pl.pallas_call(functools.partial(kernel, (n, n_mp, tuple(order), tiles, w...  59.7 us
    unnamed x1, local copies, waits for them, and re-layouts  1.77 us

profile of v2, /device:TPU:1, one launch (start us, length us, event | category | flops | bytes accessed | tf_op | source)
XLA Modules:
  0.0 61.5 jit_solution(14091011212104016764)
XLA Ops:
  0.0 59.7 %shard_map.82 = bf16[96,2048]{1,0:T(8,128)(2,1)} custom-call(s32[8]{0:T(128)} %len_ref.1, s32[8,16]{1,0:T(8,128)} %table_ref.1, bf16[1,96,16,128]{3,2,1,0:T(8,128)(2,1)} %q_ref.1, bf16[1,96,2,128]{3,2,1,0:T(2,128)(2,1)} %nk_ref.1, bf16[1,96,2,128]{3,2,1,0:T(2,128)(2,1)} %nv_ref.1, bf16[16,2,128,128]{3,2,1,0:T(8,128)(2,1)} %pk_ref.1, ...), custom_call_target="tpu_custom_call" | custom-call | tf_op jit(solution)/shard_map/pallas_call | solution.py:265
  59.7 1.8 %copy.10 = bf16[1,96,2048]{2,1,0:T(8,128)(2,1)} copy(bf16[1,96,2048]{2,1,0:T(8,128)(2,1)} %bitcast.1) | data formatting | bytes 786432

commit v3 on v2

--- a/solution.py
+++ b/solution.py
@@ -27,9 +27,9 @@
 
 
 def kernel(
-    dims, len_ref, table_ref, q_ref, nk_ref, nv_ref, pk_ref, pv_ref, w_hbm, out_ref,
-    wbuf, q32, n32, qs, sendk, sendv, recvk, recvv, probs, peaks, sums, acc, attn, sbuf, rbuf,
-    w_sem, ks_sem, kr_sem, vs_sem, vr_sem, rs_sem, rr_sem,
+    dims, len_ref, table_ref, nk_ref, nv_ref, q_hbm, pk_hbm, pv_hbm, w_hbm, out_ref,
+    pk_ref, pv_ref, q_ref, wbuf, q32, n32, qs, sendk, sendv, recvk, recvv, probs, peaks, sums, acc, attn, sbuf, rbuf,
+    in_sem, w_sem, ks_sem, kr_sem, vs_sem, vr_sem, rs_sem, rr_sem,
 ):
     n, n_mp, order, tiles, width = dims
     fresh = q_ref.shape[1]
@@ -41,14 +41,15 @@
     mz = lax.axis_index("mp")
     coef = math.log2(math.e) / math.sqrt(hd)
 
+    loads = [
+        pltpu.make_async_copy(src, dst, in_sem.at[i])
+        for i, (src, dst) in enumerate(((pk_hbm, pk_ref), (pv_hbm, pv_ref), (q_hbm, q_ref)))
+    ]
+
     def w_copy(pos, t):
         col = pl.multiple_of((flipped(mz, order[pos]) * tiles + t) * width, 128)
         i = pos * tiles + t
         return pltpu.make_async_copy(w_hbm.at[:, pl.ds(col, width)], wbuf.at[i], w_sem.at[i])
-
-    for pos in range(n_mp):
-        for t in range(tiles):
-            w_copy(pos, t).start()
 
     steps = []
     bit = 1
@@ -64,6 +65,8 @@
         pl.semaphore_signal(
             barrier, inc=1, device_id={"mp": flipped(mz, bit)}, device_id_type=MESH
         )
+    for load in loads:
+        load.start()
     pl.semaphore_wait(barrier, n - 1 + len(steps))
 
     def scan(row, owner):
@@ -105,8 +108,14 @@
             for j in range(kvh):
                 recv[me, j, s] = pool[ids[s], j]
 
+    loads[0].wait()
     send_all(pk_ref, sendk, recvk, True)
+    loads[1].wait()
     send_all(pv_ref, sendv, recvv, False)
+    loads[2].wait()
+    for pos in range(n_mp):
+        for t in range(tiles):
+            w_copy(pos, t).start()
 
     q32[...] = q_ref[0].astype(jnp.float32)
     n32[0] = nk_ref[0].astype(jnp.float32)
@@ -265,9 +274,12 @@
     out = pl.pallas_call(
         functools.partial(kernel, (n, n_mp, tuple(order), tiles, width)),
         out_shape=jax.ShapeDtypeStruct((fresh, chunk), bf16),
-        in_specs=[smem, smem] + [vmem] * 5 + [pl.BlockSpec(memory_space=pl.ANY)],
+        in_specs=[smem, smem, vmem, vmem] + [pl.BlockSpec(memory_space=pl.ANY)] * 4,
         out_specs=vmem,
         scratch_shapes=[
+            pltpu.VMEM(pool_keys.shape, bf16),
+            pltpu.VMEM(pool_values.shape, bf16),
+            pltpu.VMEM(queries.shape, bf16),
             pltpu.VMEM((n_mp * tiles, depth, width), bf16),
             pltpu.VMEM((fresh, heads, hd), f32),
             pltpu.VMEM((2, fresh, kvh, hd), f32),
@@ -283,6 +295,7 @@
             pltpu.VMEM((fresh, depth), bf16),
             pltpu.VMEM((n_mp, tiles, fresh, width), bf16),
             pltpu.VMEM((n_mp, tiles, fresh, width), bf16),
+            dma((3,)),
             dma((n_mp * tiles,)),
             dma((n,)), dma((n,)), dma((n,)), dma((n,)),
             dma((n_mp, tiles)), dma((n_mp, tiles)),
@@ -293,9 +306,9 @@
     )(
         prefix_len,
         page_table,
-        queries,
         new_keys,
         new_values,
+        queries,
         pool_keys,
         pool_values,
         out_weight,

time: 61.7 us -> 60.8 us (0.985)
  Pallas kernels: 59.7 us -> 58.8 us
    pallas_call x1, Pallas kernels: 59.7 us -> 58.8 us  [on_device(): pl.pallas_call(functools.partial(kernel, (n, n_mp, tuple(order), tiles, w...]
where the time goes in v3:
time: 60.8 us; the launch traced here: 60.6 us
  Pallas kernels  58.8 us (97%)
  local copies, waits for them, and re-layouts  1.77 us (3%)
    pallas_call x1, Pallas kernels, on_device(): pl.pallas_call(functools.partial(kernel, (n, n_mp, tuple(order), tiles, w...  58.8 us
    unnamed x1, local copies, waits for them, and re-layouts  1.77 us

profile of v3, /device:TPU:1, one launch (start us, length us, event | category | flops | bytes accessed | tf_op | source)
XLA Modules:
  0.0 60.6 jit_solution(10601507337001968643)
XLA Ops:
  0.0 58.8 %shard_map.82 = bf16[96,2048]{1,0:T(8,128)(2,1)} custom-call(s32[8]{0:T(128)} %len_ref.1, s32[8,16]{1,0:T(8,128)} %table_ref.1, bf16[1,96,2,128]{3,2,1,0:T(2,128)(2,1)} %nk_ref.1, bf16[1,96,2,128]{3,2,1,0:T(2,128)(2,1)} %nv_ref.1, bf16[1,96,16,128]{3,2,1,0:T(8,128)(2,1)} %q_hbm.1, bf16[16,2,128,128]{3,2,1,0:T(8,128)(2,1)} %pk_hbm.1, ...), custom_call_target="tpu_custom_call" | custom-call | tf_op jit(solution)/shard_map/pallas_call | solution.py:274
  58.8 1.8 %copy.10 = bf16[1,96,2048]{2,1,0:T(8,128)(2,1)} copy(bf16[1,96,2048]{2,1,0:T(8,128)(2,1)} %bitcast.1) | data formatting | bytes 786432

commit v4 on v3

--- a/solution.py
+++ b/solution.py
@@ -265,7 +265,7 @@
     chunk = model // n_mp
     width = min(512, chunk)
     tiles = chunk // width
-    order = sorted(range(n_mp), key=lambda r: (low_bit(r) if r else n_mp, -r))
+    order = range(n_mp - 1, -1, -1)
     bf16, f32 = jnp.bfloat16, jnp.float32
     dma = pltpu.SemaphoreType.DMA
     vmem = pl.BlockSpec(memory_space=pltpu.VMEM)

time: 60.8 us -> 60.8 us (level)
  no operation moved by 1% of the time
where the time goes in v4:
time: 60.8 us; the launch traced here: 60.6 us
  Pallas kernels  58.8 us (97%)
  local copies, waits for them, and re-layouts  1.77 us (3%)
    pallas_call x1, Pallas kernels, on_device(): pl.pallas_call(functools.partial(kernel, (n, n_mp, tuple(order), tiles, w...  58.8 us
    unnamed x1, local copies, waits for them, and re-layouts  1.77 us

profile of v4, /device:TPU:1, one launch (start us, length us, event | category | flops | bytes accessed | tf_op | source)
XLA Modules:
  0.0 60.6 jit_solution(13726220468345828748)
XLA Ops:
  0.0 58.8 %shard_map.82 = bf16[96,2048]{1,0:T(8,128)(2,1)} custom-call(s32[8]{0:T(128)} %len_ref.1, s32[8,16]{1,0:T(8,128)} %table_ref.1, bf16[1,96,2,128]{3,2,1,0:T(2,128)(2,1)} %nk_ref.1, bf16[1,96,2,128]{3,2,1,0:T(2,128)(2,1)} %nv_ref.1, bf16[1,96,16,128]{3,2,1,0:T(8,128)(2,1)} %q_hbm.1, bf16[16,2,128,128]{3,2,1,0:T(8,128)(2,1)} %pk_hbm.1, ...), custom_call_target="tpu_custom_call" | custom-call | tf_op jit(solution)/shard_map/pallas_call | solution.py:274
  58.8 1.8 %copy.10 = bf16[1,96,2048]{2,1,0:T(8,128)(2,1)} copy(bf16[1,96,2048]{2,1,0:T(8,128)(2,1)} %bitcast.1) | data formatting | bytes 786432
